TPU v7x, 32 devices: a whole 2x2x4 slice. The times are simulated.
32 devices in a mesh: tm: 4 (over y, core), space: 8 (over z, x).
Axes of the slice: x: 2, y: 2, z: 4, core: 2. Of those that a mesh axis runs over, the one named last changes fastest.
Arguments:
- latent: bfloat16 [32, 32, 64, 256], P('tm', 'space'), may hold values from -6 to 6
- spatial_weight: bfloat16 [3, 3, 256, 256], replicated, may hold values from -0.125 to 0.125
- spatial_bias: float32 [256], replicated, may hold values from -3 to 3
- temporal_weight: bfloat16 [3, 256, 256], replicated, may hold values from -0.21875 to 0.21875
- temporal_bias: float32 [256], replicated, may hold values from -3 to 3
Outputs:
- upsampled: bfloat16 [32, 64, 128, 256], P(('tm', 'space'))
All inputs are finite; a program needn't handle non-finite values.
Results may differ from a plain program's by a relative error of at most 0.0032.
Values may be sent and summed in bfloat16 or wider, within the bound.
No kernel may reach another device: no remote copies, remote signals or barrier semaphores. Data moves between devices by JAX's collectives and lax.ppermute only.
A program may use at most 128 MiB of HBM per device.

v0:
```python
import jax
import jax.numpy as jnp
from jax import lax
from jax.sharding import PartitionSpec as P


def padded(cells, sides, width):
    for axis, dim in sides:
        count = lax.axis_size(axis)
        ends = count - 1
        head = lax.slice_in_dim(cells, 0, width, axis=dim)
        tail = lax.slice_in_dim(cells, cells.shape[dim] - width, cells.shape[dim], axis=dim)
        cells = jnp.concatenate(
            [
                lax.ppermute(tail, axis, [(i, (i + 1) % count) for i in range(ends)]),
                cells,
                lax.ppermute(head, axis, [((i + 1) % count, i) for i in range(ends)]),
            ],
            axis=dim,
        )
    return cells


def from_behind(block, axis, distance):
    devices = range(lax.axis_size(axis))
    route = [(i - distance, i) for i in devices if i - distance in devices]
    return lax.ppermute(block, axis, route)


def temporal_mix(earlier, hidden, latent, temporal_weight, temporal_bias):
    count, rows, cols, chans = hidden.shape
    joined = jnp.concatenate([earlier, hidden], axis=0)
    total = jnp.zeros((count * rows * cols, chans), jnp.float32)
    for k in range(3):
        piece = joined[k : k + count].reshape(count * rows * cols, chans)
        total = total + jnp.dot(piece, temporal_weight[k], preferred_element_type=jnp.float32)
    own = latent.reshape(count * rows * cols, chans).astype(jnp.float32)
    return (own + total + temporal_bias).astype(jnp.bfloat16).reshape(count, rows, cols, chans)


def body(latent, spatial_weight, spatial_bias, temporal_weight, temporal_bias):
    frames, rows, cols, chans = latent.shape
    bordered = padded(latent, (("space", 1),), 1)
    bordered = jnp.pad(bordered, ((0, 0), (0, 0), (1, 1), (0, 0)))
    total = jnp.zeros((frames * rows * cols, chans), jnp.float32)
    for a in range(3):
        for b in range(3):
            tile = bordered[:, a : a + rows, b : b + cols, :].reshape(frames * rows * cols, chans)
            total = total + jnp.dot(tile, spatial_weight[a, b], preferred_element_type=jnp.float32)
    hidden = (
        jax.nn.silu(total + spatial_bias).astype(jnp.bfloat16).reshape(frames, rows, cols, chans)
    )
    earlier = from_behind(hidden[frames - 2 :], "tm", 1)
    local_mixed = temporal_mix(earlier, hidden, latent, temporal_weight, temporal_bias)
    mixed = lax.all_to_all(local_mixed, "space", split_axis=0, concat_axis=1, tiled=True)
    count, height, width, depth = mixed.shape
    grown = jnp.broadcast_to(mixed[:, :, None, :, None, :], (count, height, 2, width, 2, depth))
    return grown.reshape(count, 2 * height, 2 * width, depth)


def solution(mesh):
    in_specs = (P("tm", "space", None, None), P(), P(), P(), P())
    out_specs = P(("tm", "space"), None, None, None)
    return jax.shard_map(body, mesh=mesh, in_specs=in_specs, out_specs=out_specs, check_vma=False)
```

profile of v0, /device:TPU:1, one launch (start us, length us, event | category | flops | bytes accessed | tf_op | source)
XLA Modules:
  0.0 77.4 jit_solution(11071638202679942732)
XLA Ops:
  0.0 1.1 %fusion.40 = (bf16[8,1,64,256]{3,2,1,0:T(8,128)(2,1)S(1)}, bf16[8,1,64,256]{3,2,1,0:T(8,128)(2,1)S(1)}) fusion(bf16[8,4,64,256]{3,2,1,0:T(8,128)(2,1)} %param.5), kind=kLoop, calls=%fused_computation.57 | loop fusion | bytes 1048576 | tf_op jit(solution)/shard_map/slice | solution.py:12
  1.1 4.0 %collective-permute-start = (bf16[8,1,64,256]{3,2,1,0:T(8,128)(2,1)S(1)}, bf16[8,1,64,256]{3,2,1,0:T(8,128)(2,1)S(1)}, u32[]{:S(2)}, u32[]{:S(2)}) collective-permute-start(bf16[8,1,64,256]{3,2,1,0:T(8,128)(2,1)S(1)} %get-tuple-element.15), channel_id=1, source_target_pairs={{0,1},{1,2},{2,3},{3,4},{4,5},{5,6},{6,7},{8,9},{9,10},{10,11},{11... | collective-permute-start | bytes 786440 | tf_op jit(solution)/shard_map/ppermute | solution.py:15
  5.0 1.3 %collective-permute-start.1 = (bf16[8,1,64,256]{3,2,1,0:T(8,128)(2,1)S(1)}, bf16[8,1,64,256]{3,2,1,0:T(8,128)(2,1)S(1)}, u32[]{:S(2)}, u32[]{:S(2)}) collective-permute-start(bf16[8,1,64,256]{3,2,1,0:T(8,128)(2,1)S(1)} %get-tuple-element.16), channel_id=1, source_target_pairs={{1,0},{2,1},{3,2},{4,3},{5,4},{6,5},{7,6},{9,8},{10,9},{11,10},{12... | collective-permute-start | bytes 786440 | tf_op jit(solution)/shard_map/ppermute | solution.py:17
  6.3 3.5 %collective-permute-done = bf16[8,1,64,256]{3,2,1,0:T(8,128)(2,1)S(1)} collective-permute-done((bf16[8,1,64,256]{3,2,1,0:T(8,128)(2,1)S(1)}, bf16[8,1,64,256]{3,2,1,0:T(8,128)(2,1)S(1)}, u32[]{:S(2)}, u32[]{:S(2)}) %collective-permute-start) | collective-permute-done | bytes 262176 | tf_op jit(solution)/shard_map/ppermute | solution.py:15
  9.9 3.9 %collective-permute-done.1 = bf16[8,1,64,256]{3,2,1,0:T(8,128)(2,1)S(1)} collective-permute-done((bf16[8,1,64,256]{3,2,1,0:T(8,128)(2,1)S(1)}, bf16[8,1,64,256]{3,2,1,0:T(8,128)(2,1)S(1)}, u32[]{:S(2)}, u32[]{:S(2)}) %collective-permute-start.1) | collective-permute-done | bytes 262176 | tf_op jit(solution)/shard_map/ppermute | solution.py:17
  13.8 2.1 %fusion.10 = bf16[8,6,66,256]{3,2,1,0:T(8,128)(2,1)S(1)} fusion(bf16[8,1,64,256]{3,2,1,0:T(8,128)(2,1)S(1)} %collective-permute-done.1, bf16[8,4,64,256]{3,2,1,0:T(8,128)(2,1)} %param.5, bf16[8,1,64,256]{3,2,1,0:T(8,128)(2,1)S(1)} %collective-permute-done), kind=kLoop, calls=%fused_computation.22 | loop fusion | flops 9732096 | bytes 3194880 | tf_op jit(solution)/shard_map/concatenate | solution.py:13
  15.9 0.0 copy-start.1
  16.0 1.2 %fusion.39 = (bf16[8,4,64,256]{3,2,1,0:T(8,128)(2,1)S(1)}, bf16[8,4,64,256]{3,2,1,0:T(8,128)(2,1)S(1)}, bf16[8,4,64,256]{3,2,1,0:T(8,128)(2,1)S(1)}, bf16[8,4,64...) fusion(bf16[8,6,66,256]{3,2,1,0:T(8,128)(2,1)S(1)} %fusion.10), kind=kLoop, calls=%fused_computation.56 | loop fusion | bytes 12582912 | tf_op jit(solution)/shard_map/slice | solution.py:48
  17.2 0.0 copy-done.1
  17.2 0.4 fusion.25
  17.6 0.0 copy-start
  17.7 0.4 fusion.16
  18.1 0.8 %copy-done = bf16[8,4,64,256]{3,2,1,0:T(8,128)(2,1)S(1)} copy-done((bf16[8,4,64,256]{3,2,1,0:T(8,128)(2,1)S(1)}, bf16[8,4,64,256]{3,2,1,0:T(8,128)(2,1)}, u32[]{:S(2)}) %copy-start) | copy-done | bytes 1048600
  18.9 0.2 pad_maximum_fusion.1
  19.0 0.4 convolution_add_fusion.8
  19.5 0.4 convolution_add_fusion.7
  19.9 0.4 convolution_add_fusion.6
  20.4 0.4 convolution_add_fusion.5
  20.8 0.4 convolution_add_fusion.4
  21.2 0.0 copy-start.4
  21.3 0.4 convolution_add_fusion.3
  21.7 0.2 copy-done.4
  21.9 0.8 %multiply_convert_fusion = bf16[2048,256]{1,0:T(8,128)(2,1)S(1)} fusion(f32[2048,256]{1,0:T(8,128)S(1)} %fusion.16, f32[2048,256]{1,0:T(8,128)S(1)} %convolution_add_fusion.3, bf16[2048,256]{1,0:T(8,128)(2,1)S(1)} %bitcast.77, f32[256]{0:T(256)S(1)} %copy-done.4, bf16[3,3,256,256]{3,2,1,0:T(8,128)(2,1)S(1)} %copy-done.1), kind=kOutput, calls=%fused_computation.17 | convolution fusion | flops 272629760 | bytes 6423552 | tf_op jit(solution)/shard_map/dot_general | solution.py:49
  22.8 0.0 copy-start.2
  22.8 6.5 %collective-permute-start.2 = (bf16[2,4,64,256]{3,2,1,0:T(8,128)(2,1)S(1)}, bf16[2,4,64,256]{3,2,1,0:T(8,128)(2,1)S(1)}, u32[]{:S(2)}, u32[]{:S(2)}) collective-permute-start(bf16[2,4,64,256]{3,2,1,0:T(8,128)(2,1)S(1)} %bitcast.78), channel_id=1, source_target_pairs={{0,8},{8,16},{16,24},{1,9},{9,17},{17,25},{2,10},{10,18},{18,26},{... | collective-permute-start | bytes 786440 | tf_op jit(solution)/shard_map/ppermute | solution.py:27
  29.3 3.3 %collective-permute-done.2 = bf16[2,4,64,256]{3,2,1,0:T(8,128)(2,1)S(1)} collective-permute-done((bf16[2,4,64,256]{3,2,1,0:T(8,128)(2,1)S(1)}, bf16[2,4,64,256]{3,2,1,0:T(8,128)(2,1)S(1)}, u32[]{:S(2)}, u32[]{:S(2)}) %collective-permute-start.2) | collective-permute-done | bytes 262176 | tf_op jit(solution)/shard_map/ppermute | solution.py:27
  32.6 0.1 fusion.11
  32.7 0.0 copy-done.2
  32.8 0.4 fusion.13
  33.2 0.0 copy-start.3
  33.2 0.5 convolution_add_fusion.1
  33.7 0.2 copy-done.3
  33.9 0.5 fusion.5
  34.4 29.8 %all_to_all.4 = bf16[8,4,64,256]{3,2,1,0:T(8,128)(2,1)S(1)} all-to-all(bf16[8,4,64,256]{3,2,1,0:T(8,128)(2,1)S(1)} %bitcast.76), channel_id=1, replica_groups=mesh['tm'=4,'space'=8] {'space'}, dimensions={0} | all-to-all | bytes 2097152 | tf_op jit(solution)/shard_map/all_to_all | solution.py:55
  64.2 6.0 %broadcast_in_dim.13 = bf16[32,2,64,2,256]{4,3,2,1,0:T(2,128)(2,1)} broadcast(bf16[32,64,256]{2,1,0:T(8,128)(2,1)S(1)} %bitcast.69), dimensions={0,2,4} | broadcast | bytes 5242880 | tf_op jit(solution)/shard_map/broadcast_in_dim | solution.py:57
  70.2 7.2 %broadcast_in_dim.14 = bf16[1,64,128,256]{3,2,1,0:T(8,128)(2,1)} reshape(bf16[32,2,64,2,256]{4,3,2,1,0:T(2,128)(2,1)} %broadcast_in_dim.13) | data formatting | bytes 8388608 | tf_op jit(solution)/shard_map/broadcast_in_dim | solution.py:57
  (1 shorter events, 0.0 us)
Async XLA Ops:
  1.1 8.8 %collective-permute-start = (bf16[8,1,64,256]{3,2,1,0:T(8,128)(2,1)S(1)}, bf16[8,1,64,256]{3,2,1,0:T(8,128)(2,1)S(1)}, u32[]{:S(2)}, u32[]{:S(2)}) collective-permute-start(bf16[8,1,64,256]{3,2,1,0:T(8,128)(2,1)S(1)} %get-tuple-element.15), channel_id=1, source_target_pairs={{0,1},{1,2},{2,3},{3,4},{4,5},{5,6},{6,7},{8,9},{9,10},{10,11},{11... | collective-permute-start | bytes 786440 | tf_op jit(solution)/shard_map/ppermute | solution.py:15
  5.0 8.8 %collective-permute-start.1 = (bf16[8,1,64,256]{3,2,1,0:T(8,128)(2,1)S(1)}, bf16[8,1,64,256]{3,2,1,0:T(8,128)(2,1)S(1)}, u32[]{:S(2)}, u32[]{:S(2)}) collective-permute-start(bf16[8,1,64,256]{3,2,1,0:T(8,128)(2,1)S(1)} %get-tuple-element.16), channel_id=1, source_target_pairs={{1,0},{2,1},{3,2},{4,3},{5,4},{6,5},{7,6},{9,8},{10,9},{11,10},{12... | collective-permute-start | bytes 786440 | tf_op jit(solution)/shard_map/ppermute | solution.py:17
  15.9 1.3 %copy-start.1 = (bf16[3,3,256,256]{3,2,1,0:T(8,128)(2,1)S(1)}, bf16[3,3,256,256]{3,2,1,0:T(8,128)(2,1)}, u32[]{:S(2)}) copy-start(bf16[3,3,256,256]{3,2,1,0:T(8,128)(2,1)} %param.6) | copy-start | bytes 3538948
  17.6 1.2 %copy-start = (bf16[8,4,64,256]{3,2,1,0:T(8,128)(2,1)S(1)}, bf16[8,4,64,256]{3,2,1,0:T(8,128)(2,1)}, u32[]{:S(2)}) copy-start(bf16[8,4,64,256]{3,2,1,0:T(8,128)(2,1)} %param.5) | copy-start | bytes 3145732
  21.2 0.7 copy-start.4
  22.8 10.0 %copy-start.2 = (bf16[3,256,256]{2,1,0:T(8,128)(2,1)S(1)}, bf16[3,256,256]{2,1,0:T(8,128)(2,1)}, u32[]{:S(2)}) copy-start(bf16[3,256,256]{2,1,0:T(8,128)(2,1)} %param.8) | copy-start | bytes 1179652
  22.8 9.8 %collective-permute-start.2 = (bf16[2,4,64,256]{3,2,1,0:T(8,128)(2,1)S(1)}, bf16[2,4,64,256]{3,2,1,0:T(8,128)(2,1)S(1)}, u32[]{:S(2)}, u32[]{:S(2)}) collective-permute-start(bf16[2,4,64,256]{3,2,1,0:T(8,128)(2,1)S(1)} %bitcast.78), channel_id=1, source_target_pairs={{0,8},{8,16},{16,24},{1,9},{9,17},{17,25},{2,10},{10,18},{18,26},{... | collective-permute-start | bytes 786440 | tf_op jit(solution)/shard_map/ppermute | solution.py:27
  33.2 0.7 copy-start.3
where the time goes:
time: 77.9 us; the launch traced here: 77.4 us
  blocking collectives  29.8 us (38%)
  local copies, waits for them, and re-layouts  16.8 us (22%)
  starting transfers between devices  11.8 us (15%)
  waiting for transfers between devices  10.7 us (14%)
  matrix products  5.67 us (7%)
  other arithmetic  2.43 us (3%)
    all_to_all x1, blocking collectives, body(): lax.all_to_all(local_mixed, 'space', split_axis=0, concat_axis=1, tiled=T...  29.8 us
    broadcast_in_dim x2, local copies, waits for them, and re-layouts, body(): jnp.broadcast_to(mixed[:, :, None, :, None, :], (count, height, 2, width,...  13.2 us
    ppermute x1, starting transfers between devices, from_behind(): return lax.ppermute(block, axis, route)  6.52 us
    dot_general x9, matrix products, body(): jnp.dot(tile, spatial_weight[a, b], preferred_element_type=jnp.float32)  4.29 us
    ppermute x1, starting transfers between devices, padded(): lax.ppermute(tail, axis, [(i, (i + 1) % count) for i in range(ends)])  3.96 us
    ppermute x1, waiting for transfers between devices, padded(): lax.ppermute(head, axis, [((i + 1) % count, i) for i in range(ends)])  3.94 us
    ppermute x1, waiting for transfers between devices, padded(): lax.ppermute(tail, axis, [(i, (i + 1) % count) for i in range(ends)])  3.51 us
    ppermute x1, waiting for transfers between devices, from_behind(): return lax.ppermute(block, axis, route)  3.29 us
  transfers between devices with their start and end apart: 3, of which 3 were waited for; matrix products, arithmetic and copies ran while one was open for 0% of the time, Pallas kernels for 0%

commit v1 on v0

--- a/solution.py
+++ b/solution.py
@@ -52,7 +52,12 @@
     )
     earlier = from_behind(hidden[frames - 2 :], "tm", 1)
     local_mixed = temporal_mix(earlier, hidden, latent, temporal_weight, temporal_bias)
-    mixed = lax.all_to_all(local_mixed, "space", split_axis=0, concat_axis=1, tiled=True)
+    mixed = jnp.concatenate(
+        lax.all_to_all(
+            jnp.stack(jnp.split(local_mixed, lax.axis_size("space"), axis=0)), "space", 0, 0
+        ),
+        axis=1,
+    )
     count, height, width, depth = mixed.shape
     grown = jnp.broadcast_to(mixed[:, :, None, :, None, :], (count, height, 2, width, 2, depth))
     return grown.reshape(count, 2 * height, 2 * width, depth)

time: 77.9 us -> 78.2 us (level)
  no operation moved by 1% of the time
where the time goes in v1:
time: 78.2 us; the launch traced here: 77.7 us
  blocking collectives  29.8 us (38%)
  local copies, waits for them, and re-layouts  17 us (22%)
  starting transfers between devices  11.8 us (15%)
  waiting for transfers between devices  10.7 us (14%)
  matrix products  5.74 us (7%)
  other arithmetic  2.43 us (3%)
    all_to_all x1, blocking collectives, body(): lax.all_to_all(jnp.stack(jnp.split(local_mixed, lax.axis_size('space'), a...  29.8 us
    broadcast_in_dim x2, local copies, waits for them, and re-layouts, body(): jnp.broadcast_to(mixed[:, :, None, :, None, :], (count, height, 2, width,...  13.2 us
    ppermute x1, starting transfers between devices, from_behind(): return lax.ppermute(block, axis, route)  6.52 us
    dot_general x9, matrix products, body(): jnp.dot(tile, spatial_weight[a, b], preferred_element_type=jnp.float32)  4.32 us
    ppermute x1, starting transfers between devices, padded(): lax.ppermute(tail, axis, [(i, (i + 1) % count) for i in range(ends)])  3.96 us
    ppermute x1, waiting for transfers between devices, padded(): lax.ppermute(head, axis, [((i + 1) % count, i) for i in range(ends)])  3.94 us
    ppermute x1, waiting for transfers between devices, padded(): lax.ppermute(tail, axis, [(i, (i + 1) % count) for i in range(ends)])  3.51 us
    ppermute x1, waiting for transfers between devices, from_behind(): return lax.ppermute(block, axis, route)  3.29 us
  transfers between devices with their start and end apart: 3, of which 3 were waited for; matrix products, arithmetic and copies ran while one was open for 0% of the time, Pallas kernels for 0%

profile of v1, /device:TPU:1, one launch (start us, length us, event | category | flops | bytes accessed | tf_op | source)
XLA Modules:
  0.0 77.7 jit_solution(9905253987468928053)
XLA Ops:
  0.0 1.1 %fusion.41 = (bf16[8,1,64,256]{3,2,1,0:T(8,128)(2,1)S(1)}, bf16[8,1,64,256]{3,2,1,0:T(8,128)(2,1)S(1)}) fusion(bf16[8,4,64,256]{3,2,1,0:T(8,128)(2,1)} %param.5), kind=kLoop, calls=%fused_computation.66 | loop fusion | bytes 1048576 | tf_op jit(solution)/shard_map/slice | solution.py:12
  1.1 4.0 %collective-permute-start = (bf16[8,1,64,256]{3,2,1,0:T(8,128)(2,1)S(1)}, bf16[8,1,64,256]{3,2,1,0:T(8,128)(2,1)S(1)}, u32[]{:S(2)}, u32[]{:S(2)}) collective-permute-start(bf16[8,1,64,256]{3,2,1,0:T(8,128)(2,1)S(1)} %get-tuple-element.23), channel_id=1, source_target_pairs={{0,1},{1,2},{2,3},{3,4},{4,5},{5,6},{6,7},{8,9},{9,10},{10,11},{11... | collective-permute-start | bytes 786440 | tf_op jit(solution)/shard_map/ppermute | solution.py:15
  5.0 1.3 %collective-permute-start.1 = (bf16[8,1,64,256]{3,2,1,0:T(8,128)(2,1)S(1)}, bf16[8,1,64,256]{3,2,1,0:T(8,128)(2,1)S(1)}, u32[]{:S(2)}, u32[]{:S(2)}) collective-permute-start(bf16[8,1,64,256]{3,2,1,0:T(8,128)(2,1)S(1)} %get-tuple-element.24), channel_id=1, source_target_pairs={{1,0},{2,1},{3,2},{4,3},{5,4},{6,5},{7,6},{9,8},{10,9},{11,10},{12... | collective-permute-start | bytes 786440 | tf_op jit(solution)/shard_map/ppermute | solution.py:17
  6.3 3.5 %collective-permute-done = bf16[8,1,64,256]{3,2,1,0:T(8,128)(2,1)S(1)} collective-permute-done((bf16[8,1,64,256]{3,2,1,0:T(8,128)(2,1)S(1)}, bf16[8,1,64,256]{3,2,1,0:T(8,128)(2,1)S(1)}, u32[]{:S(2)}, u32[]{:S(2)}) %collective-permute-start) | collective-permute-done | bytes 262176 | tf_op jit(solution)/shard_map/ppermute | solution.py:15
  9.8 3.9 %collective-permute-done.1 = bf16[8,1,64,256]{3,2,1,0:T(8,128)(2,1)S(1)} collective-permute-done((bf16[8,1,64,256]{3,2,1,0:T(8,128)(2,1)S(1)}, bf16[8,1,64,256]{3,2,1,0:T(8,128)(2,1)S(1)}, u32[]{:S(2)}, u32[]{:S(2)}) %collective-permute-start.1) | collective-permute-done | bytes 262176 | tf_op jit(solution)/shard_map/ppermute | solution.py:17
  13.8 2.1 %fusion.10 = bf16[8,6,66,256]{3,2,1,0:T(8,128)(2,1)S(1)} fusion(bf16[8,1,64,256]{3,2,1,0:T(8,128)(2,1)S(1)} %collective-permute-done.1, bf16[8,4,64,256]{3,2,1,0:T(8,128)(2,1)} %param.5, bf16[8,1,64,256]{3,2,1,0:T(8,128)(2,1)S(1)} %collective-permute-done), kind=kLoop, calls=%fused_computation.22 | loop fusion | flops 9732096 | bytes 3194880 | tf_op jit(solution)/shard_map/concatenate | solution.py:13
  15.9 0.0 copy-start.1
  15.9 1.3 %fusion.39 = (bf16[8,4,64,256]{3,2,1,0:T(8,128)(2,1)S(1)}, bf16[8,4,64,256]{3,2,1,0:T(8,128)(2,1)S(1)}, bf16[8,4,64,256]{3,2,1,0:T(8,128)(2,1)S(1)}, bf16[8,4,64...) fusion(bf16[8,6,66,256]{3,2,1,0:T(8,128)(2,1)S(1)} %fusion.10), kind=kLoop, calls=%fused_computation.64 | loop fusion | bytes 12582912 | tf_op jit(solution)/shard_map/slice | solution.py:48
  17.3 0.0 copy-done.1
  17.3 0.4 fusion.25
  17.7 0.0 copy-start
  17.7 0.4 fusion.16
  18.2 0.8 %copy-done = bf16[8,4,64,256]{3,2,1,0:T(8,128)(2,1)S(1)} copy-done((bf16[8,4,64,256]{3,2,1,0:T(8,128)(2,1)S(1)}, bf16[8,4,64,256]{3,2,1,0:T(8,128)(2,1)}, u32[]{:S(2)}) %copy-start) | copy-done | bytes 1048600
  18.9 0.2 pad_maximum_fusion.1
  19.1 0.4 convolution_add_fusion.8
  19.5 0.4 convolution_add_fusion.7
  20.0 0.4 convolution_add_fusion.6
  20.4 0.5 convolution_add_fusion.5
  20.9 0.4 convolution_add_fusion.4
  21.3 0.0 copy-start.4
  21.3 0.4 convolution_add_fusion.3
  21.8 0.2 copy-done.4
  22.0 0.8 %multiply_convert_fusion = bf16[2048,256]{1,0:T(8,128)(2,1)S(1)} fusion(f32[2048,256]{1,0:T(8,128)S(1)} %fusion.16, f32[2048,256]{1,0:T(8,128)S(1)} %convolution_add_fusion.3, bf16[2048,256]{1,0:T(8,128)(2,1)S(1)} %bitcast.83, f32[256]{0:T(256)S(1)} %copy-done.4, bf16[3,3,256,256]{3,2,1,0:T(8,128)(2,1)S(1)} %copy-done.1), kind=kOutput, calls=%fused_computation.17 | convolution fusion | flops 272629760 | bytes 6423552 | tf_op jit(solution)/shard_map/dot_general | solution.py:49
  22.8 0.0 copy-start.2
  22.9 6.5 %collective-permute-start.2 = (bf16[2,4,64,256]{3,2,1,0:T(8,128)(2,1)S(1)}, bf16[2,4,64,256]{3,2,1,0:T(8,128)(2,1)S(1)}, u32[]{:S(2)}, u32[]{:S(2)}) collective-permute-start(bf16[2,4,64,256]{3,2,1,0:T(8,128)(2,1)S(1)} %bitcast.92), channel_id=1, source_target_pairs={{0,8},{8,16},{16,24},{1,9},{9,17},{17,25},{2,10},{10,18},{18,26},{... | collective-permute-start | bytes 786440 | tf_op jit(solution)/shard_map/ppermute | solution.py:27
  29.4 3.3 %collective-permute-done.2 = bf16[2,4,64,256]{3,2,1,0:T(8,128)(2,1)S(1)} collective-permute-done((bf16[2,4,64,256]{3,2,1,0:T(8,128)(2,1)S(1)}, bf16[2,4,64,256]{3,2,1,0:T(8,128)(2,1)S(1)}, u32[]{:S(2)}, u32[]{:S(2)}) %collective-permute-start.2) | collective-permute-done | bytes 262176 | tf_op jit(solution)/shard_map/ppermute | solution.py:27
  32.7 0.1 fusion.11
  32.8 0.0 copy-done.2
  32.8 0.4 fusion.13
  33.3 0.0 copy-start.3
  33.3 0.5 convolution_add_fusion.1
  33.8 0.2 copy-done.3
  34.0 0.5 fusion.5
  34.5 0.1 fusion.40
  34.7 29.8 %all_to_all.5 = bf16[8,1,4,64,256]{4,3,2,1,0:T(8,128)(2,1)S(1)} all-to-all(bf16[8,1,4,64,256]{4,3,2,1,0:T(8,128)(2,1)S(1)} %constant_dynamic-update-slice_fusion), channel_id=1, replica_groups=mesh['tm'=4,'space'=8] {'space'}, dimensions={0} | all-to-all | bytes 2097152 | tf_op jit(solution)/shard_map/all_to_all | solution.py:56
  64.5 6.0 %broadcast_in_dim.12 = bf16[32,2,64,2,256]{4,3,2,1,0:T(2,128)(2,1)} broadcast(bf16[32,64,256]{2,1,0:T(8,128)(2,1)S(1)} %bitcast.76), dimensions={0,2,4} | broadcast | bytes 5242880 | tf_op jit(solution)/shard_map/broadcast_in_dim | solution.py:62
  70.5 7.2 %broadcast_in_dim.13 = bf16[1,64,128,256]{3,2,1,0:T(8,128)(2,1)} reshape(bf16[32,2,64,2,256]{4,3,2,1,0:T(2,128)(2,1)} %broadcast_in_dim.12) | data formatting | bytes 8388608 | tf_op jit(solution)/shard_map/broadcast_in_dim | solution.py:62
  (9 shorter events, 0.1 us)
Async XLA Ops:
  1.1 8.8 %collective-permute-start = (bf16[8,1,64,256]{3,2,1,0:T(8,128)(2,1)S(1)}, bf16[8,1,64,256]{3,2,1,0:T(8,128)(2,1)S(1)}, u32[]{:S(2)}, u32[]{:S(2)}) collective-permute-start(bf16[8,1,64,256]{3,2,1,0:T(8,128)(2,1)S(1)} %get-tuple-element.23), channel_id=1, source_target_pairs={{0,1},{1,2},{2,3},{3,4},{4,5},{5,6},{6,7},{8,9},{9,10},{10,11},{11... | collective-permute-start | bytes 786440 | tf_op jit(solution)/shard_map/ppermute | solution.py:15
  5.0 8.8 %collective-permute-start.1 = (bf16[8,1,64,256]{3,2,1,0:T(8,128)(2,1)S(1)}, bf16[8,1,64,256]{3,2,1,0:T(8,128)(2,1)S(1)}, u32[]{:S(2)}, u32[]{:S(2)}) collective-permute-start(bf16[8,1,64,256]{3,2,1,0:T(8,128)(2,1)S(1)} %get-tuple-element.24), channel_id=1, source_target_pairs={{1,0},{2,1},{3,2},{4,3},{5,4},{6,5},{7,6},{9,8},{10,9},{11,10},{12... | collective-permute-start | bytes 786440 | tf_op jit(solution)/shard_map/ppermute | solution.py:17
  15.9 1.3 %copy-start.1 = (bf16[3,3,256,256]{3,2,1,0:T(8,128)(2,1)S(1)}, bf16[3,3,256,256]{3,2,1,0:T(8,128)(2,1)}, u32[]{:S(2)}) copy-start(bf16[3,3,256,256]{3,2,1,0:T(8,128)(2,1)} %param.6) | copy-start | bytes 3538948
  17.7 1.2 %copy-start = (bf16[8,4,64,256]{3,2,1,0:T(8,128)(2,1)S(1)}, bf16[8,4,64,256]{3,2,1,0:T(8,128)(2,1)}, u32[]{:S(2)}) copy-start(bf16[8,4,64,256]{3,2,1,0:T(8,128)(2,1)} %param.5) | copy-start | bytes 3145732
  21.3 0.7 copy-start.4
  22.8 10.0 %copy-start.2 = (bf16[3,256,256]{2,1,0:T(8,128)(2,1)S(1)}, bf16[3,256,256]{2,1,0:T(8,128)(2,1)}, u32[]{:S(2)}) copy-start(bf16[3,256,256]{2,1,0:T(8,128)(2,1)} %param.8) | copy-start | bytes 1179652
  22.9 9.8 %collective-permute-start.2 = (bf16[2,4,64,256]{3,2,1,0:T(8,128)(2,1)S(1)}, bf16[2,4,64,256]{3,2,1,0:T(8,128)(2,1)S(1)}, u32[]{:S(2)}, u32[]{:S(2)}) collective-permute-start(bf16[2,4,64,256]{3,2,1,0:T(8,128)(2,1)S(1)} %bitcast.92), channel_id=1, source_target_pairs={{0,8},{8,16},{16,24},{1,9},{9,17},{17,25},{2,10},{10,18},{18,26},{... | collective-permute-start | bytes 786440 | tf_op jit(solution)/shard_map/ppermute | solution.py:27
  33.3 0.7 copy-start.3
